TPU v7x, 512 devices: a whole 4x4x16 slice. The times are simulated.
512 devices in a mesh: fib: 16 (over y, x), blk: 32 (over z, core).
Axes of the slice: x: 4, y: 4, z: 16, core: 2. Of those that a mesh axis runs over, the one named last changes fastest.
Arguments:
- field_data: float32 [33, 64, 512, 256], P(None, 'blk', 'fib'), may hold values from -120 to 120
- start_block: float32 [512, 64], replicated, may hold values from -6 to 6
Outputs:
- core_out: float32 [33, 64, 64, 256], P(None, 'blk', 'fib')
All inputs are finite; a program needn't handle non-finite values.
Results may differ from a plain program's by a relative error of at most 0.00013.
Values sent between devices are 32-bit elements; how exact they have to be, the bound alone decides.
A program may use at most 192 MiB of HBM per device.

v0:
```python
import jax
import jax.numpy as jnp
from jax import lax
from jax.sharding import PartitionSpec as P


def shards(field_data, start_block):
    highest = lax.Precision.HIGHEST
    received = lax.all_to_all(field_data, "fib", split_axis=3, concat_axis=2, tiled=True)
    width_x = received.shape[2]
    unfolded = jnp.transpose(received, (0, 1, 3, 2)).reshape(-1, width_x)
    contract_rows = (((0,), (0,)), ((), ()))
    local_gram = lax.dot_general(unfolded, unfolded, contract_rows, precision=highest)
    gram_total = lax.psum(local_gram, ("fib", "blk"))
    raw_basis = jnp.dot(gram_total, start_block, precision=highest)
    inner_block = jnp.dot(raw_basis.T, raw_basis, precision=highest)
    lower_factor = jnp.linalg.cholesky(inner_block)
    basis_cols = jax.scipy.linalg.solve_triangular(lower_factor, raw_basis.T, lower=True).T
    core_local = jnp.einsum("szxy,xr->szry", received, basis_cols, precision=highest)
    return lax.all_to_all(core_local, "fib", split_axis=2, concat_axis=3, tiled=True)


def solution(mesh):
    in_specs = (P(None, "blk", "fib", None), P())
    out_specs = P(None, "blk", "fib", None)
    return jax.shard_map(shards, mesh=mesh, in_specs=in_specs, out_specs=out_specs, check_vma=False)
```

profile of v0, /device:TPU:1, one launch (start us, length us, event | category | flops | bytes accessed | tf_op | source)
XLA Modules:
  0.0 619.4 jit_solution(7491580162648552195)
XLA Ops:
  6.5 0.0 copy-start
  6.5 0.0 all-reduce.2.cloned.1.call-start
  6.5 8.7 %copy.13 = f32[33,2,32,256]{0,2,1,3:T(8,128)} copy(f32[33,2,32,256]{3,2,1,0:T(8,128)} %param.2) | data formatting | bytes 4325376 | tf_op args[0]
  15.2 10.1 %reshape.13 = f32[16,1,33792]{2,1,0:T(1,128)S(1)} reshape(f32[256,2,32,33]{3,2,1,0:T(8,128)} %bitcast.45) | data formatting | bytes 4325376
  25.3 34.1 %all_to_all.36 = f32[16,1,33792]{2,1,0:T(1,128)} all-to-all(f32[16,1,33792]{2,1,0:T(1,128)S(1)} %reshape.13), channel_id=1, replica_groups=mesh['fib'=16,'blk'=32] {'fib'}, dimensions={0} | all-to-all | bytes 4325376 | tf_op jit(solution)/shard_map/all_to_all | solution.py:9
  59.4 0.5 broadcast.53
  59.9 7.4 %reduce.6 = f32[16,33792]{1,0:T(8,128)S(1)} reduce(f32[16,1,33792]{2,1,0:T(1,128)} %all_to_all.36, f32[]{:T(128)} %broadcast.53), dimensions={1}, to_apply=%all_to_all.26.reduce_sub_computation | reduce | bytes 4325380 | tf_op jit(solution)/shard_map/all_to_all | solution.py:9
  67.3 12.4 %reshape.14 = f32[256,2,32,33]{3,2,1,0:T(8,128)} reshape(f32[16,33792]{1,0:T(8,128)S(1)} %reduce.6) | data formatting | bytes 4325376
  79.8 11.7 %copy.15 = f32[33,2,16,32,16]{3,2,4,1,0:T(8,128)} copy(f32[33,2,16,32,16]{0,3,1,4,2:T(8,128)} %bitcast.46) | data formatting | bytes 4325376 | tf_op jit(solution)/shard_map/all_to_all | solution.py:9
  91.5 6.7 %all_to_all.29 = f32[33,2,512,16]{2,3,1,0:T(8,128)S(1)} reshape(f32[33,2,16,32,16]{3,2,4,1,0:T(8,128)} %copy.15) | data formatting | bytes 4325376 | tf_op jit(solution)/shard_map/all_to_all | solution.py:9
  98.2 5.4 fusion.4
  103.5 0.0 all-reduce.2.cloned.1.call-update
  103.6 470.4 %all-reduce.2.cloned.1.call-done = f32[512,512]{1,0:T(8,128)} async-done(((f32[512,512]{1,0:T(8,128)}), f32[512,512]{1,0:T(8,128)}) %all-reduce.2.cloned.1.call-update) | async-done | bytes 1048592 | tf_op jit(solution)/shard_map/psum | solution.py:14
  574.0 0.0 copy-done
  574.0 2.4 fusion.13
  576.4 0.3 fusion.14
  576.6 0.1 copy.16
  576.7 5.8 cholesky.16
  582.6 0.7 compare_reduce_fusion
  583.3 0.7 fusion.10
  584.0 4.9 custom-call.7
  588.9 0.3 convolution_bitcast_fusion
  589.3 3.0 fusion.7
  592.3 1.0 copy.18
  593.3 1.0 reshape.15
  594.3 14.6 %all_to_all.37 = f32[16,1,4224]{2,1,0:T(1,128)S(1)} all-to-all(f32[16,1,4224]{2,1,0:T(1,128)S(1)} %reshape.15), channel_id=1, replica_groups=mesh['fib'=16,'blk'=32] {'fib'}, dimensions={0} | all-to-all | bytes 540672 | tf_op jit(solution)/shard_map/all_to_all | solution.py:20
  608.9 1.3 reduce.7
  610.2 1.1 reshape.16
  611.4 0.1 copy.20
  611.5 1.0 copy.21
  (2 shorter events, 0.0 us)
Async XLA Ops:
  6.5 567.5 %copy-start = (f32[512,64]{0,1:T(8,128)S(1)}, f32[512,64]{0,1:T(8,128)}, u32[]{:S(2)}) copy-start(f32[512,64]{0,1:T(8,128)} %param.3) | copy-start | bytes 393220
  6.5 567.5 %all-reduce.2.cloned.1.call-start = ((), (), s32[]{:S(2)}) async-start(), calls=%async_computation.2 | async-start | bytes 2097152 | tf_op jit(solution)/shard_map/psum | solution.py:14
Sparse Core Ops, SparseCore 0:
  103.7 470.2 all-reduce.1
where the time goes:
time: 620 us; the launch traced here: 619 us
  waiting for transfers between devices  470 us (76%)
  local copies, waits for them, and re-layouts  54.5 us (9%)
  blocking collectives  48.7 us (8%)
  other arithmetic  20.9 us (3%)
  between operations  13.5 us (2%)
  matrix products  11.3 us (2%)
    psum x1, waiting for transfers between devices, shards(): gram_total = lax.psum(local_gram, ('fib', 'blk'))  470 us
    all_to_all x1, blocking collectives, shards(): lax.all_to_all(field_data, 'fib', split_axis=3, concat_axis=2, tiled=True)  34.1 us
    unnamed x7, local copies, waits for them, and re-layouts  33.4 us
    all_to_all x3, local copies, waits for them, and re-layouts, shards(): lax.all_to_all(field_data, 'fib', split_axis=3, concat_axis=2, tiled=True)  18.9 us
    all_to_all x1, blocking collectives, shards(): lax.all_to_all(core_local, 'fib', split_axis=2, concat_axis=3, tiled=True)  14.6 us
  transfers between devices with their start and end apart: 1, of which 1 were waited for; matrix products, arithmetic and copies ran while one was open for 0% of the time, Pallas kernels for 0%

commit v1 on v0

v1 whole, which is shorter than its diff:
```python
import functools

import jax
import jax.numpy as jnp
from jax import lax
from jax.experimental import pallas as pl
from jax.experimental.pallas import tpu as pltpu
from jax.sharding import PartitionSpec as P

MESH = pl.DeviceIdType.MESH
HIGHEST = lax.Precision.HIGHEST
CORES = 2
NT = (((1,), (1,)), ((), ()))


def owner_of(unit, shift, side):
    if side == 4:
        return unit * 4 + lax.rem(unit + shift, 4)
    return unit


def eliminate(inner, rank):
    wide = inner.shape[1]
    rows = lax.broadcasted_iota(jnp.int32, (rank, wide), 0)
    lanes = lax.broadcasted_iota(jnp.int32, (rank, wide), 1)
    augmented = jnp.where(lanes == rows + rank, 1.0, inner)
    blocks = [augmented[8 * i : 8 * i + 8, :] for i in range(rank // 8)]
    sub = lax.broadcasted_iota(jnp.int32, (8, 1), 0)
    for k in range(rank):
        kb, kr = divmod(k, 8)
        pivot_row = blocks[kb][kr : kr + 1, :]
        scaled = pivot_row * (1.0 / pivot_row[:, k : k + 1])
        for i in range(kb, rank // 8):
            column = blocks[i][:, k : k + 1]
            if i == kb:
                column = jnp.where(sub > kr, column, 0.0)
            blocks[i] = blocks[i] - column * scaled
    reduced = jnp.concatenate(blocks, axis=0)
    pivots = jnp.sum(jnp.where(lanes == rows, reduced, 0.0), axis=1, keepdims=True)
    return reduced * (1.0 / jnp.sqrt(pivots))


def kernel(nf, nz, field, start, out, fbuf, lbuf, part, rbuf, zsrc, zbuf, gsrc, gbuf, osrc, lsrc,
           a_send, a_recv, own_sem, l_send, l_recv, r_send, r_recv, z_send, z_recv, g_send, g_recv,
           o_send, o_recv, p_send, p_recv, own_out):
    side = {16: 4, 4: 2}[nf]
    width_x = field.shape[2]
    rank = start.shape[1]
    last = field.shape[0] - 1
    plane = nf * CORES
    f = lax.axis_index("fib")
    b = lax.axis_index("blk")
    core, z = lax.rem(b, CORES), lax.div(b, CORES)
    t = f * CORES + core
    row, col = lax.div(f, side), lax.rem(f, side)
    shift = lax.rem(b, 4)

    def plane_peer(k):
        other = lax.rem(t + k, plane)
        return other, {"fib": lax.div(other, CORES), "blk": z * CORES + lax.rem(other, CORES)}

    def z_peer(k):
        return {"fib": f, "blk": lax.rem(z + k, nz) * CORES + core}

    def fib_peer(k):
        return lax.rem(row + lax.div(k, side), side) * side + lax.rem(col + lax.rem(k, side), side)

    barrier = pltpu.get_barrier_semaphore()

    def greet_plane(k, _):
        pl.semaphore_signal(barrier, inc=1, device_id=plane_peer(k)[1], device_id_type=MESH)
        return 0

    def greet_z(k, _):
        pl.semaphore_signal(barrier, inc=1, device_id=z_peer(k), device_id_type=MESH)
        return 0

    lax.fori_loop(1, plane, greet_plane, 0)
    lax.fori_loop(1, nz, greet_z, 0)
    own = pltpu.make_async_copy(
        field.at[pl.ds(2 * f, 2)], fbuf.at[:, :, pl.ds(pl.multiple_of(f * width_x, width_x), width_x), :], own_sem)
    own.start()
    pl.semaphore_wait(barrier, plane - 1 + nz - 1)

    mine = pl.ds(pl.multiple_of(f * width_x, width_x), width_x)
    for u in range(4):
        owner = owner_of(u, shift, side)
        source = field.at[last, u // 2, :, pl.ds((u % 2) * 128, 128)]

        @pl.when(owner != f)
        def _():
            pltpu.make_async_remote_copy(source, lbuf.at[mine, :], l_send, l_recv, {"fib": owner, "blk": b}, MESH).start()

        @pl.when(owner == f)
        def _():
            pltpu.make_async_copy(source, lbuf.at[mine, :], own_out).start()

    for q in range(4):
        def send_pair(k, _, q=q):
            peer = fib_peer(k)
            pltpu.make_async_remote_copy(
                field.at[2 * peer + q // 2, q % 2], fbuf.at[q // 2, q % 2, mine, :], a_send, a_recv.at[q],
                {"fib": peer, "blk": b}, MESH).start()
            return 0

        lax.fori_loop(1, nf, send_pair, 0)

    others = pl.ds(0, (nf - 1) * width_x)
    start_t = jnp.transpose(start[...])
    own.wait()
    raw = jnp.zeros((start.shape[0], rank), jnp.float32)
    for q in range(4):
        whole = fbuf.at[q // 2, q % 2]
        pltpu.make_async_copy(whole.at[others, :], whole.at[others, :], a_recv.at[q]).wait()
        fibres = whole[...]
        projected = jnp.dot(start_t, fibres, precision=HIGHEST, preferred_element_type=jnp.float32)
        raw = raw + lax.dot_general(fibres, projected, NT, precision=HIGHEST, preferred_element_type=jnp.float32)
    raw_t = jnp.transpose(raw)
    tiles_x = start.shape[0] // 128
    for i in range(rank // 8):
        for j in range(tiles_x):
            part[i * tiles_x + j] = raw_t[8 * i : 8 * i + 8, 128 * j : 128 * j + 128]

    row_unit = row if side == 4 else f
    is_owner = owner_of(row_unit, shift, side) == f

    @pl.when(is_owner)
    def _():
        pltpu.make_async_copy(lbuf.at[others, :], lbuf.at[others, :], l_recv).wait()
        pltpu.make_async_copy(lbuf.at[mine, :], lbuf.at[mine, :], own_out).wait()
        fibres = lbuf[...]
        projected = jnp.dot(start_t, fibres, precision=HIGHEST, preferred_element_type=jnp.float32)
        extra = jnp.transpose(
            lax.dot_general(fibres, projected, NT, precision=HIGHEST, preferred_element_type=jnp.float32))
        for i in range(rank // 8):
            for j in range(tiles_x):
                part[i * tiles_x + j] += extra[8 * i : 8 * i + 8, 128 * j : 128 * j + 128]

    def scatter(k, _):
        other, device = plane_peer(k)
        pltpu.make_async_remote_copy(part.at[other], rbuf.at[t], r_send, r_recv, device, MESH).start()
        return 0

    lax.fori_loop(1, plane, scatter, 0)
    rbuf[t] = part[t]
    rest = pl.ds(0, plane - 1)
    pltpu.make_async_copy(rbuf.at[rest], rbuf.at[rest], r_recv).wait()
    tile = jnp.sum(rbuf[...], axis=0)
    zsrc[...] = tile
    zbuf[z] = tile

    def exchange(k, _):
        pltpu.make_async_remote_copy(zsrc, zbuf.at[z], z_send, z_recv, z_peer(k), MESH).start()
        return 0

    lax.fori_loop(1, nz, exchange, 0)
    rest_z = pl.ds(0, nz - 1)
    pltpu.make_async_copy(zbuf.at[rest_z], zbuf.at[rest_z], z_recv).wait()
    tile = jnp.sum(zbuf[...], axis=0)
    gsrc[...] = tile
    gbuf[t] = tile

    def gather(k, _):
        pltpu.make_async_remote_copy(gsrc, gbuf.at[t], g_send, g_recv, plane_peer(k)[1], MESH).start()
        return 0

    lax.fori_loop(1, plane, gather, 0)
    pltpu.make_async_copy(gbuf.at[rest], gbuf.at[rest], g_recv).wait()
    total_t = jnp.concatenate(
        [jnp.concatenate([gbuf[i * tiles_x + j] for j in range(tiles_x)], axis=1) for i in range(rank // 8)], axis=0)

    padding = jnp.zeros((128 - rank, total_t.shape[1]), jnp.float32)
    inner = lax.dot_general(total_t, jnp.concatenate([total_t, padding], axis=0), NT, precision=HIGHEST,
                            preferred_element_type=jnp.float32)
    inverse = eliminate(inner, rank)
    pieces = [jnp.zeros((rank, total_t.shape[1]), jnp.float32), total_t]
    if 128 - 2 * rank:
        pieces.append(jnp.zeros((128 - 2 * rank, total_t.shape[1]), jnp.float32))
    basis_t = jnp.dot(inverse, jnp.concatenate(pieces, axis=0), precision=HIGHEST, preferred_element_type=jnp.float32)

    share = rank // nf
    for s in range(2):
        for zz in range(2):
            core_part = jnp.dot(basis_t, fbuf[s, zz], precision=HIGHEST, preferred_element_type=jnp.float32)
            for j in range(nf):
                osrc[j, s, zz] = core_part[share * j : share * j + share, :]

        def send_core(k, _, s=s):
            peer = fib_peer(k)
            pltpu.make_async_remote_copy(osrc.at[peer, s], out.at[2 * f + s], o_send, o_recv,
                                         {"fib": peer, "blk": b}, MESH).start()
            return 0

        lax.fori_loop(1, nf, send_core, 0)
    own_core = pltpu.make_async_copy(osrc.at[f], out.at[pl.ds(2 * f, 2)], own_sem)
    own_core.start()

    @pl.when(is_owner)
    def _():
        core_part = jnp.dot(basis_t, lbuf[...], precision=HIGHEST, preferred_element_type=jnp.float32)
        for j in range(nf):
            lsrc[j] = core_part[share * j : share * j + share, :]
        lanes = pl.ds(pl.multiple_of(lax.rem(row_unit, 2) * 128, 128), 128)
        target = out.at[last, lax.div(row_unit, 2), :, lanes]

        def send_last(k, _):
            peer = fib_peer(k)
            pltpu.make_async_remote_copy(lsrc.at[peer], target, p_send, p_recv, {"fib": peer, "blk": b}, MESH).start()
            return 0

        lax.fori_loop(1, nf, send_last, 0)
        own_last = pltpu.make_async_copy(lsrc.at[f], target, own_out)
        own_last.start()
        own_last.wait()

    own_core.wait()
    arrived = out.at[pl.ds(0, 2 * (nf - 1))]
    pltpu.make_async_copy(arrived, arrived, o_recv).wait()
    pltpu.make_async_copy(arrived, arrived, o_send).wait()
    sent = fbuf.at[:, :, others, :]
    pltpu.make_async_copy(sent, sent, a_send).wait()
    pltpu.make_async_copy(rbuf.at[rest], rbuf.at[rest], r_send).wait()
    pltpu.make_async_copy(zbuf.at[rest_z], zbuf.at[rest_z], z_send).wait()
    pltpu.make_async_copy(gbuf.at[rest], gbuf.at[rest], g_send).wait()

    def finish_last(owned):
        units = 4 - owned
        pltpu.make_async_copy(lsrc.at[pl.ds(0, units)], lsrc.at[pl.ds(0, units)], p_recv).wait()
        slab = lbuf.at[pl.ds(0, units * width_x), :]
        pltpu.make_async_copy(slab, slab, l_send).wait()

    @pl.when(is_owner)
    def _():
        finish_last(1)
        pltpu.make_async_copy(lsrc.at[pl.ds(0, nf - 1)], lsrc.at[pl.ds(0, nf - 1)], p_send).wait()

    if side == 4:
        @pl.when(jnp.logical_not(is_owner))
        def _():
            finish_last(0)


def solution(mesh):
    nf, nb = mesh.shape["fib"], mesh.shape["blk"]
    nz = nb // CORES

    def shards(field_data, start_block):
        species, planes, width_x, width_y = field_data.shape
        full_x, rank = start_block.shape
        share = rank // nf
        tiles = rank * full_x // 1024
        assert species == 2 * nf + 1 and planes == 2 and width_y == 256 and tiles == nf * CORES and 2 * rank <= 128
        f32 = jnp.float32
        dma = pltpu.SemaphoreType.DMA
        return pl.pallas_call(
            functools.partial(kernel, nf, nz),
            out_shape=jax.ShapeDtypeStruct((species, planes, share, width_y), f32),
            in_specs=[pl.BlockSpec(memory_space=pl.ANY), pl.BlockSpec(memory_space=pltpu.VMEM)],
            out_specs=pl.BlockSpec(memory_space=pl.ANY),
            scratch_shapes=[
                pltpu.VMEM((2, 2, full_x, width_y), f32),
                pltpu.VMEM((full_x, 128), f32),
                pltpu.VMEM((tiles, 8, 128), f32),
                pltpu.VMEM((tiles, 8, 128), f32),
                pltpu.VMEM((8, 128), f32),
                pltpu.VMEM((nz, 8, 128), f32),
                pltpu.VMEM((8, 128), f32),
                pltpu.VMEM((tiles, 8, 128), f32),
                pltpu.VMEM((nf, 2, 2, share, width_y), f32),
                pltpu.VMEM((nf, share, 128), f32),
                dma, dma((4,)), dma, dma, dma, dma, dma, dma, dma, dma, dma, dma, dma, dma, dma, dma,
            ],
            compiler_params=pltpu.CompilerParams(collective_id=0, has_side_effects=True, vmem_limit_bytes=48 << 20),
            cost_estimate=pl.CostEstimate(flops=2_000_000_000, bytes_accessed=5_000_000, transcendentals=64),
            name="hosvd_step",
        )(field_data, start_block)

    in_specs = (P(None, "blk", "fib", None), P())
    out_specs = P(None, "blk", "fib", None)
    return jax.shard_map(shards, mesh=mesh, in_specs=in_specs, out_specs=out_specs, check_vma=False)
```

time: 620 us -> 80.1 us (0.13)
  waiting for transfers between devices: 470 us -> 0 us
  Pallas kernels: 0 us -> 76.5 us
  local copies, waits for them, and re-layouts: 54.5 us -> 3.34 us
  blocking collectives: 48.7 us -> 0 us
  other arithmetic: 20.9 us -> 0 us
  between operations: 13.5 us -> 0.03 us
  matrix products: 11.3 us -> 0 us
    psum x1 -> x0, waiting for transfers between devices: 470 us -> none  [shards(): gram_total = lax.psum(local_gram, ('fib', 'blk'))]
    pallas_call x0 -> x1, Pallas kernels: none -> 76.5 us  [shards(): pl.pallas_call(functools.partial(kernel, nf, nz), out_shape=jax.ShapeDtyp...]
    all_to_all x2 -> x0, blocking collectives: 48.7 us -> none  [the longest x1 34.1 us: shards(): lax.all_to_all(field_data, 'fib', split_axis=3, concat_axis=2, tiled=True)]
    unnamed x7 -> x4, local copies, waits for them, and re-layouts: 33.4 us -> 3.34 us
    all_to_all x5 -> x0, local copies, waits for them, and re-layouts: 20 us -> none  [the longest x3 18.9 us: shards(): lax.all_to_all(field_data, 'fib', split_axis=3, concat_axis=2, tiled=True)]
    another operation x5 -> x0, other arithmetic: 12.2 us -> none  [the longest x3 6.6 us: shards(): lower_factor = jnp.linalg.cholesky(inner_block)]
    dot_general x4 -> x0, matrix products: 11 us -> none  [the longest x1 5.37 us: shards(): lax.dot_general(unfolded, unfolded, contract_rows, precision=highest)]
    all_to_all x2 -> x0, other arithmetic: 8.67 us -> none  [the longest x1 7.4 us: shards(): lax.all_to_all(field_data, 'fib', split_axis=3, concat_axis=2, tiled=True)]
  transfers between devices with their start and end apart: 1 -> 0, of which waited for: 1 -> 0; matrix products, arithmetic and copies ran while one was open for 0% -> 0% of each run, Pallas kernels for 0% -> 0%
where the time goes in v1:
time: 80.1 us; the launch traced here: 79.9 us
  Pallas kernels  76.5 us (96%)
  local copies, waits for them, and re-layouts  3.34 us (4%)
    pallas_call x1, Pallas kernels, shards(): pl.pallas_call(functools.partial(kernel, nf, nz), out_shape=jax.ShapeDtyp...  76.5 us
    unnamed x4, local copies, waits for them, and re-layouts  3.34 us

profile of v1, /device:TPU:1, one launch (start us, length us, event | category | flops | bytes accessed | tf_op | source)
XLA Modules:
  0.0 79.9 jit_solution(7570880907112928134)
XLA Ops:
  0.0 1.0 %copy.3.start = f32[512,64]{1,0:T(8,128)S(1)} copy(f32[512,64]{0,1:T(8,128)} %param.3) | data formatting | bytes 262144 | tf_op args[1]
  1.0 0.0 copy-start
  1.0 1.6 %copy-done = f32[33,2,32,256]{3,2,1,0:T(8,128)S(1)} copy-done((f32[33,2,32,256]{3,2,1,0:T(8,128)S(1)}, f32[33,2,32,256]{3,2,1,0:T(8,128)}, u32[]{:S(2)}) %copy-start) | copy-done | bytes 2162712
  2.6 76.5 %hosvd_step.1 = f32[33,2,4,256]{3,2,1,0:T(4,128)S(1)} custom-call(f32[33,2,32,256]{3,2,1,0:T(8,128)S(1)} %copy-done, f32[512,64]{1,0:T(8,128)S(1)} %copy.3.start), custom_call_target="tpu_custom_call" | custom-call | flops 2000000000 | bytes 5000000 | tf_op jit(solution)/shard_map/hosvd_step/pallas_call | solution.py:255
  79.2 0.7 copy.5
Async XLA Ops:
  1.0 1.6 %copy-start = (f32[33,2,32,256]{3,2,1,0:T(8,128)S(1)}, f32[33,2,32,256]{3,2,1,0:T(8,128)}, u32[]{:S(2)}) copy-start(f32[33,2,32,256]{3,2,1,0:T(8,128)} %field.1) | copy-start | bytes 6488068

commit v2 on v1

v2 whole, which is shorter than its diff:
```python
import functools

import jax
import jax.numpy as jnp
from jax import lax
from jax.experimental import pallas as pl
from jax.experimental.pallas import tpu as pltpu
from jax.sharding import PartitionSpec as P

MESH = pl.DeviceIdType.MESH
HIGHEST = lax.Precision.HIGHEST
CORES = 2
NT = (((1,), (1,)), ((), ()))


def owner_of(unit, shift, side):
    if side == 4:
        return unit * 4 + lax.rem(unit + shift, 4)
    return unit


def ring_distance(step, size):
    return min(step % size, -step % size)


def eliminate(inner, rank):
    wide = inner.shape[1]
    rows = lax.broadcasted_iota(jnp.int32, (rank, wide), 0)
    lanes = lax.broadcasted_iota(jnp.int32, (rank, wide), 1)
    augmented = jnp.where(lanes == rows + rank, 1.0, inner)
    blocks = [augmented[8 * i : 8 * i + 8, :] for i in range(rank // 8)]
    sub = lax.broadcasted_iota(jnp.int32, (8, wide), 0)

    def columns(block, p):
        return [jnp.broadcast_to(block[:, 8 * p + m : 8 * p + m + 1], (8, wide)) for m in range(8)]

    for p in range(rank // 8):
        panel, block = columns(blocks[p], p), blocks[p]
        pivot_rows, factors = [], []
        for j in range(8):
            inv = 1.0 / panel[j][j : j + 1, :]
            pivot_rows.append(block[j : j + 1, :] * inv)
            factors.append([panel[m][j : j + 1, :] * inv for m in range(j + 1, 8)])
            below = jnp.where(sub > j, panel[j], 0.0)
            block = block - below * pivot_rows[j]
            for m in range(j + 1, 8):
                panel[m] = panel[m] - below * factors[j][m - j - 1]
        blocks[p] = block
        for i in range(p + 1, rank // 8):
            panel, block = columns(blocks[i], p), blocks[i]
            for j in range(8):
                block = block - panel[j] * pivot_rows[j]
                for m in range(j + 1, 8):
                    panel[m] = panel[m] - panel[j] * factors[j][m - j - 1]
            blocks[i] = block
    reduced = jnp.concatenate(blocks, axis=0)
    pivots = jnp.sum(jnp.where(lanes == rows, reduced, 0.0), axis=1, keepdims=True)
    return reduced * (1.0 / jnp.sqrt(pivots))


def halves(value):
    high = value.astype(jnp.bfloat16)
    return high, (value - high.astype(jnp.float32)).astype(jnp.bfloat16)


def kernel(nf, nz, field, start_hbm, out, start_t, fbuf, lbuf, fhigh, flow, lhigh, llow, part, extra, rbuf, zsrc, zbuf,
           gsrc, gbuf, osrc, lsrc, a_send, a_recv, own_sem, start_sem, l_send, l_recv, own_last, r_send, r_recv, z_send,
           z_recv, g_send, g_recv, o_send, o_recv, p_send, p_recv):
    side = {16: 4, 4: 2}[nf]
    width_x = field.shape[2]
    rank, full_x = start_t.shape
    last = field.shape[0] - 1
    plane = nf * CORES
    f = lax.axis_index("fib")
    b = lax.axis_index("blk")
    core, z = lax.rem(b, CORES), lax.div(b, CORES)
    t = f * CORES + core
    row, col = lax.div(f, side), lax.rem(f, side)
    shift = lax.rem(b, 4)
    row_unit = row if side == 4 else f
    is_owner = owner_of(row_unit, shift, side) == f
    mine = pl.ds(pl.multiple_of(f * width_x, width_x), width_x)
    others = pl.ds(0, (nf - 1) * width_x)

    own = pltpu.make_async_copy(field.at[pl.ds(2 * f, 2)], fbuf.at[:, :, mine, :], own_sem)
    own.start()
    start_copy = pltpu.make_async_copy(start_hbm, start_t, start_sem)
    start_copy.start()

    steps = [(dy, dx) for dy in range(side) for dx in range(side)]
    steps.sort(key=lambda s: -ring_distance(s[0], side) - ring_distance(s[1], side))
    row_at = [lax.rem(row + d, side) * side for d in range(side)]
    col_at = [lax.rem(col + d, side) for d in range(side)]
    fibs = [row_at[dy] + col_at[dx] for dy, dx in steps]
    fib_peers = fibs[:-1]
    twin = z * CORES + 1 - core
    plane_peers = []
    for other in fibs:
        if other is not fibs[-1]:
            plane_peers.append((other * CORES + core, {"fib": other, "blk": b}))
        plane_peers.append((other * CORES + 1 - core, {"fib": other, "blk": twin}))
    z_steps = sorted(range(1, nz), key=lambda k: -ring_distance(k, nz))
    z_peers = [{"fib": f, "blk": lax.rem(z + k, nz) * CORES + core} for k in z_steps]

    barrier = pltpu.get_barrier_semaphore()
    for other in fib_peers:
        pl.semaphore_signal(barrier, inc=1, device_id={"fib": other, "blk": b}, device_id_type=MESH)
    for device in z_peers:
        pl.semaphore_signal(barrier, inc=1, device_id=device, device_id_type=MESH)
    for other in fibs:
        pl.semaphore_signal(barrier, inc=1, device_id={"fib": other, "blk": twin}, device_id_type=MESH)
    pl.semaphore_wait(barrier, plane - 1 + nz - 1)

    for u in range(4):
        owner = owner_of(u, shift, side)
        source = field.at[last, u // 2, :, pl.ds((u % 2) * 128, 128)]

        @pl.when(owner != f)
        def _():
            pltpu.make_async_remote_copy(source, lbuf.at[mine, :], l_send, l_recv, {"fib": owner, "blk": b}, MESH).start()

        @pl.when(owner == f)
        def _():
            pltpu.make_async_copy(source, lbuf.at[mine, :], own_last).start()

    def send_pair(q, _):
        s, zz = lax.div(q, 2), lax.rem(q, 2)
        for peer in fib_peers:
            pltpu.make_async_remote_copy(
                field.at[2 * peer + s, zz], fbuf.at[s, zz, mine, :], a_send, a_recv.at[q], {"fib": peer, "blk": b}, MESH
            ).start()
        return 0

    lax.fori_loop(0, 4, send_pair, 0)

    tiles_x = full_x // 128
    tiles = [(i, j) for i in range(rank // 8) for j in range(tiles_x)]

    def gram_term(fibres):
        projected = jnp.dot(start_t[...], fibres, precision=HIGHEST, preferred_element_type=jnp.float32)
        return lax.dot_general(fibres, projected, NT, precision=HIGHEST, preferred_element_type=jnp.float32)

    extra[...] = jnp.zeros_like(extra)
    own.wait()
    start_copy.wait()
    raw = jnp.zeros((full_x, rank), jnp.float32)
    for q in range(4):
        whole = fbuf.at[q // 2, q % 2]
        pltpu.make_async_copy(whole.at[others, :], whole.at[others, :], a_recv.at[q]).wait()
        raw = raw + gram_term(whole[...])
        if q < 3:
            fhigh[q], flow[q] = halves(whole[...])
        if q == 1:
            @pl.when(is_owner)
            def _():
                pltpu.make_async_copy(lbuf.at[others, :], lbuf.at[others, :], l_recv).wait()
                pltpu.make_async_copy(lbuf.at[mine, :], lbuf.at[mine, :], own_last).wait()
                term = jnp.transpose(gram_term(lbuf[...]))
                for n, (i, j) in enumerate(tiles):
                    extra[n] = term[8 * i : 8 * i + 8, 128 * j : 128 * j + 128]
                lhigh[...], llow[...] = halves(lbuf[...])
    raw_t = jnp.transpose(raw)
    for n, (i, j) in enumerate(tiles):
        part[n] = raw_t[8 * i : 8 * i + 8, 128 * j : 128 * j + 128] + extra[n]

    for other, device in plane_peers:
        pltpu.make_async_remote_copy(part.at[other], rbuf.at[t], r_send, r_recv, device, MESH).start()
    rbuf[t] = part[t]
    fhigh[3], flow[3] = halves(fbuf[1, 1])
    rest = pl.ds(0, plane - 1)
    pltpu.make_async_copy(rbuf.at[rest], rbuf.at[rest], r_recv).wait()
    tile = jnp.sum(rbuf[...], axis=0)
    zsrc[...] = tile
    for device in z_peers:
        pltpu.make_async_remote_copy(zsrc, zbuf.at[z], z_send, z_recv, device, MESH).start()
    zbuf[z] = tile
    rest_z = pl.ds(0, nz - 1)
    pltpu.make_async_copy(zbuf.at[rest_z], zbuf.at[rest_z], z_recv).wait()
    tile = jnp.sum(zbuf[...], axis=0)
    gsrc[...] = tile
    for _, device in plane_peers:
        pltpu.make_async_remote_copy(gsrc, gbuf.at[t], g_send, g_recv, device, MESH).start()
    gbuf[t] = tile
    pltpu.make_async_copy(gbuf.at[rest], gbuf.at[rest], g_recv).wait()
    total_t = jnp.concatenate(
        [jnp.concatenate([gbuf[i * tiles_x + j] for j in range(tiles_x)], axis=1) for i in range(rank // 8)], axis=0)

    def pad(count):
        return [jnp.zeros((count, full_x), jnp.float32)] if count else []

    inner = lax.dot_general(total_t, jnp.concatenate([total_t] + pad(128 - rank), axis=0), NT, precision=HIGHEST,
                            preferred_element_type=jnp.float32)
    inverse = eliminate(inner, rank)
    basis_t = jnp.dot(inverse, jnp.concatenate(pad(rank) + [total_t] + pad(128 - 2 * rank), axis=0), precision=HIGHEST,
                      preferred_element_type=jnp.float32)
    basis_high, basis_low = halves(basis_t)
    basis_both = jnp.concatenate([basis_high, basis_low], axis=0)

    share = rank // nf

    def core_of(high, low):
        both = jnp.dot(basis_both, high, preferred_element_type=jnp.float32)
        return both[:rank] + both[rank:] + jnp.dot(basis_high, low, preferred_element_type=jnp.float32)

    @pl.when(is_owner)
    def _():
        core_part = core_of(lhigh[...], llow[...])
        for j in range(nf):
            lsrc[j] = core_part[share * j : share * j + share, :]

    for q in range(4):
        core_part = core_of(fhigh[q], flow[q])
        for j in range(nf):
            osrc[j, q // 2, q % 2] = core_part[share * j : share * j + share, :]
    target = out.at[pl.ds(2 * f, 2)]
    last_lanes = pl.ds(pl.multiple_of(lax.rem(row_unit, 2) * 128, 128), 128)
    last_target = out.at[last, lax.div(row_unit, 2), :, last_lanes]
    for peer in fib_peers:
        device = {"fib": peer, "blk": b}
        pltpu.make_async_remote_copy(osrc.at[peer], target, o_send, o_recv, device, MESH).start()

        @pl.when(is_owner)
        def _():
            pltpu.make_async_remote_copy(lsrc.at[peer], last_target, p_send, p_recv, device, MESH).start()

    own_core = pltpu.make_async_copy(osrc.at[f], target, own_sem)
    own_core.start()

    @pl.when(is_owner)
    def _():
        own_unit = pltpu.make_async_copy(lsrc.at[f], last_target, own_last)
        own_unit.start()
        own_unit.wait()

    sent = fbuf.at[:, :, others, :]
    pltpu.make_async_copy(sent, sent, a_send).wait()
    pltpu.make_async_copy(rbuf.at[rest], rbuf.at[rest], r_send).wait()
    pltpu.make_async_copy(zbuf.at[rest_z], zbuf.at[rest_z], z_send).wait()
    pltpu.make_async_copy(gbuf.at[rest], gbuf.at[rest], g_send).wait()
    own_core.wait()
    arrived = out.at[pl.ds(0, 2 * (nf - 1))]
    pltpu.make_async_copy(arrived, arrived, o_send).wait()
    pltpu.make_async_copy(arrived, arrived, o_recv).wait()

    def finish_last(units):
        slab = lbuf.at[pl.ds(0, units * width_x), :]
        pltpu.make_async_copy(slab, slab, l_send).wait()
        pltpu.make_async_copy(lsrc.at[pl.ds(0, units)], lsrc.at[pl.ds(0, units)], p_recv).wait()

    @pl.when(is_owner)
    def _():
        finish_last(3)
        pltpu.make_async_copy(lsrc.at[pl.ds(0, nf - 1)], lsrc.at[pl.ds(0, nf - 1)], p_send).wait()

    if side == 4:
        @pl.when(jnp.logical_not(is_owner))
        def _():
            finish_last(4)


def solution(mesh):
    nf, nb = mesh.shape["fib"], mesh.shape["blk"]
    nz = nb // CORES

    def shards(field_data, start_block):
        species, planes, width_x, width_y = field_data.shape
        full_x, rank = start_block.shape
        share = rank // nf
        tiles = rank * full_x // 1024
        assert species == 2 * nf + 1 and planes == 2 and width_y == 256 and tiles == nf * CORES and 2 * rank <= 128
        f32, bf16 = jnp.float32, jnp.bfloat16
        dma = pltpu.SemaphoreType.DMA
        return pl.pallas_call(
            functools.partial(kernel, nf, nz),
            out_shape=jax.ShapeDtypeStruct((species, planes, share, width_y), f32),
            in_specs=[pl.BlockSpec(memory_space=pltpu.HBM), pl.BlockSpec(memory_space=pltpu.HBM)],
            out_specs=pl.BlockSpec(memory_space=pl.ANY),
            scratch_shapes=[
                pltpu.VMEM((rank, full_x), f32),
                pltpu.VMEM((2, 2, full_x, width_y), f32),
                pltpu.VMEM((full_x, 128), f32),
                pltpu.VMEM((4, full_x, width_y), bf16),
                pltpu.VMEM((4, full_x, width_y), bf16),
                pltpu.VMEM((full_x, 128), bf16),
                pltpu.VMEM((full_x, 128), bf16),
                pltpu.VMEM((tiles, 8, 128), f32),
                pltpu.VMEM((tiles, 8, 128), f32),
                pltpu.VMEM((tiles, 8, 128), f32),
                pltpu.VMEM((8, 128), f32),
                pltpu.VMEM((nz, 8, 128), f32),
                pltpu.VMEM((8, 128), f32),
                pltpu.VMEM((tiles, 8, 128), f32),
                pltpu.VMEM((nf, 2, 2, share, width_y), f32),
                pltpu.VMEM((nf, share, 128), f32),
                dma, dma((4,)), dma, dma, dma, dma, dma, dma, dma, dma, dma, dma, dma, dma, dma, dma, dma,
            ],
            compiler_params=pltpu.CompilerParams(collective_id=0, has_side_effects=True, vmem_limit_bytes=48 << 20),
            cost_estimate=pl.CostEstimate(flops=2_000_000_000, bytes_accessed=5_000_000, transcendentals=64),
            name="hosvd_step",
        )(pltpu.with_memory_space_constraint(field_data, pltpu.HBM), pltpu.with_memory_space_constraint(start_block.T, pltpu.HBM))

    in_specs = (P(None, "blk", "fib", None), P())
    out_specs = P(None, "blk", "fib", None)
    return jax.shard_map(shards, mesh=mesh, in_specs=in_specs, out_specs=out_specs, check_vma=False)
```

time: 80.1 us -> 71.7 us (0.90)
  Pallas kernels: 76.5 us -> 70.9 us
  local copies, waits for them, and re-layouts: 3.34 us -> 0.71 us
    pallas_call x1, Pallas kernels: 76.5 us -> 70.9 us  [shards(): pl.pallas_call(functools.partial(kernel, nf, nz), out_shape=jax.ShapeDtyp...]
    unnamed x4 -> x1, local copies, waits for them, and re-layouts: 3.34 us -> 0.71 us
where the time goes in v2:
time: 71.7 us; the launch traced here: 71.6 us
  Pallas kernels  70.9 us (99%)
    pallas_call x1, Pallas kernels, shards(): pl.pallas_call(functools.partial(kernel, nf, nz), out_shape=jax.ShapeDtyp...  70.9 us

profile of v2, /device:TPU:1, one launch (start us, length us, event | category | flops | bytes accessed | tf_op | source)
XLA Modules:
  0.0 71.6 jit_solution(18407624051623440731)
XLA Ops:
  0.0 70.9 %hosvd_step.1 = f32[33,2,4,256]{3,2,1,0:T(4,128)S(1)} custom-call(f32[33,2,32,256]{3,2,1,0:T(8,128)} %field.1, f32[64,512]{1,0:T(8,128)} %bitcast.1), custom_call_target="tpu_custom_call" | custom-call | flops 2000000000 | bytes 5000000 | tf_op jit(solution)/shard_map/hosvd_step/pallas_call | solution.py:273
  70.9 0.7 copy.4

commit v3 on v2

--- a/solution.py
+++ b/solution.py
@@ -103,12 +103,10 @@
     z_peers = [{"fib": f, "blk": lax.rem(z + k, nz) * CORES + core} for k in z_steps]
 
     barrier = pltpu.get_barrier_semaphore()
-    for other in fib_peers:
-        pl.semaphore_signal(barrier, inc=1, device_id={"fib": other, "blk": b}, device_id_type=MESH)
+    for _, device in plane_peers:
+        pl.semaphore_signal(barrier, inc=1, device_id=device, device_id_type=MESH)
     for device in z_peers:
         pl.semaphore_signal(barrier, inc=1, device_id=device, device_id_type=MESH)
-    for other in fibs:
-        pl.semaphore_signal(barrier, inc=1, device_id={"fib": other, "blk": twin}, device_id_type=MESH)
     pl.semaphore_wait(barrier, plane - 1 + nz - 1)
 
     for u in range(4):
@@ -131,23 +129,31 @@
             ).start()
         return 0
 
-    lax.fori_loop(0, 4, send_pair, 0)
+    lax.fori_loop(0, 3, send_pair, 0)
+    for h in range(2):
+        lanes = pl.ds(128 * h, 128)
+        for peer in fib_peers:
+            pltpu.make_async_remote_copy(
+                field.at[2 * peer + 1, 1, :, lanes], fbuf.at[1, 1, mine, lanes], a_send, a_recv.at[3 + h],
+                {"fib": peer, "blk": b}, MESH
+            ).start()
 
     tiles_x = full_x // 128
     tiles = [(i, j) for i in range(rank // 8) for j in range(tiles_x)]
 
     def gram_term(fibres):
         projected = jnp.dot(start_t[...], fibres, precision=HIGHEST, preferred_element_type=jnp.float32)
-        return lax.dot_general(fibres, projected, NT, precision=HIGHEST, preferred_element_type=jnp.float32)
+        return lax.dot_general(projected, fibres, NT, precision=HIGHEST, preferred_element_type=jnp.float32)
 
     extra[...] = jnp.zeros_like(extra)
     own.wait()
     start_copy.wait()
-    raw = jnp.zeros((full_x, rank), jnp.float32)
-    for q in range(4):
-        whole = fbuf.at[q // 2, q % 2]
+    chunks = [(0, 0, 0, 256), (0, 1, 0, 256), (1, 0, 0, 256), (1, 1, 0, 128), (1, 1, 128, 128)]
+    raw_t = jnp.zeros((rank, full_x), jnp.float32)
+    for q, (s, zz, first, width) in enumerate(chunks):
+        whole = fbuf.at[s, zz, :, pl.ds(first, width)]
         pltpu.make_async_copy(whole.at[others, :], whole.at[others, :], a_recv.at[q]).wait()
-        raw = raw + gram_term(whole[...])
+        raw_t = raw_t + gram_term(whole[...])
         if q < 3:
             fhigh[q], flow[q] = halves(whole[...])
         if q == 1:
@@ -155,13 +161,16 @@
             def _():
                 pltpu.make_async_copy(lbuf.at[others, :], lbuf.at[others, :], l_recv).wait()
                 pltpu.make_async_copy(lbuf.at[mine, :], lbuf.at[mine, :], own_last).wait()
-                term = jnp.transpose(gram_term(lbuf[...]))
+                term = gram_term(lbuf[...])
                 for n, (i, j) in enumerate(tiles):
                     extra[n] = term[8 * i : 8 * i + 8, 128 * j : 128 * j + 128]
                 lhigh[...], llow[...] = halves(lbuf[...])
-    raw_t = jnp.transpose(raw)
+        if q == 3:
+            for n, (i, j) in enumerate(tiles):
+                part[n] = raw_t[8 * i : 8 * i + 8, 128 * j : 128 * j + 128] + extra[n]
+            raw_t = jnp.zeros((rank, full_x), jnp.float32)
     for n, (i, j) in enumerate(tiles):
-        part[n] = raw_t[8 * i : 8 * i + 8, 128 * j : 128 * j + 128] + extra[n]
+        part[n] += raw_t[8 * i : 8 * i + 8, 128 * j : 128 * j + 128]
 
     for other, device in plane_peers:
         pltpu.make_async_remote_copy(part.at[other], rbuf.at[t], r_send, r_recv, device, MESH).start()
@@ -292,7 +301,7 @@
                 pltpu.VMEM((tiles, 8, 128), f32),
                 pltpu.VMEM((nf, 2, 2, share, width_y), f32),
                 pltpu.VMEM((nf, share, 128), f32),
-                dma, dma((4,)), dma, dma, dma, dma, dma, dma, dma, dma, dma, dma, dma, dma, dma, dma, dma,
+                dma, dma((5,)), dma, dma, dma, dma, dma, dma, dma, dma, dma, dma, dma, dma, dma, dma, dma,
             ],
             compiler_params=pltpu.CompilerParams(collective_id=0, has_side_effects=True, vmem_limit_bytes=48 << 20),
             cost_estimate=pl.CostEstimate(flops=2_000_000_000, bytes_accessed=5_000_000, transcendentals=64),

time: 71.7 us -> 70.2 us (0.979)
  Pallas kernels: 70.9 us -> 69.3 us
    pallas_call x1, Pallas kernels: 70.9 us -> 69.3 us  [shards(): pl.pallas_call(functools.partial(kernel, nf, nz), out_shape=jax.ShapeDtyp...]
where the time goes in v3:
time: 70.2 us; the launch traced here: 70.1 us
  Pallas kernels  69.3 us (99%)
  local copies, waits for them, and re-layouts  0.71 us (1%)
    pallas_call x1, Pallas kernels, shards(): pl.pallas_call(functools.partial(kernel, nf, nz), out_shape=jax.ShapeDtyp...  69.3 us

profile of v3, /device:TPU:1, one launch (start us, length us, event | category | flops | bytes accessed | tf_op | source)
XLA Modules:
  0.0 70.1 jit_solution(1319556049956445991)
XLA Ops:
  0.0 69.3 %hosvd_step.1 = f32[33,2,4,256]{3,2,1,0:T(4,128)S(1)} custom-call(f32[33,2,32,256]{3,2,1,0:T(8,128)} %field.1, f32[64,512]{1,0:T(8,128)} %bitcast.1), custom_call_target="tpu_custom_call" | custom-call | flops 2000000000 | bytes 5000000 | tf_op jit(solution)/shard_map/hosvd_step/pallas_call | solution.py:282
  69.3 0.7 %copy.4 = f32[33,2,4,256]{3,2,1,0:T(4,128)} copy(f32[33,2,4,256]{3,2,1,0:T(4,128)S(1)} %hosvd_step.1) | data formatting | bytes 540672

commit v4 on v3

--- a/solution.py
+++ b/solution.py
@@ -65,7 +65,7 @@
 
 def kernel(nf, nz, field, start_hbm, out, start_t, fbuf, lbuf, fhigh, flow, lhigh, llow, part, extra, rbuf, zsrc, zbuf,
            gsrc, gbuf, osrc, lsrc, a_send, a_recv, own_sem, start_sem, l_send, l_recv, own_last, r_send, r_recv, z_send,
-           z_recv, g_send, g_recv, o_send, o_recv, p_send, p_recv):
+           z_recv, g_send, g_recv, o_send, o_recv, p_send, p_recv, plane_in, z_in):
     side = {16: 4, 4: 2}[nf]
     width_x = field.shape[2]
     rank, full_x = start_t.shape
@@ -103,11 +103,26 @@
     z_peers = [{"fib": f, "blk": lax.rem(z + k, nz) * CORES + core} for k in z_steps]
 
     barrier = pltpu.get_barrier_semaphore()
-    for _, device in plane_peers:
+    for other in fib_peers:
+        pl.semaphore_signal(barrier, inc=1, device_id={"fib": other, "blk": z * CORES}, device_id_type=MESH)
+
+    @pl.when(core == 1)
+    def _():
+        pl.semaphore_signal(barrier, inc=1, device_id={"fib": f, "blk": z * CORES}, device_id_type=MESH)
+
+    for k in z_steps:
+        device = {"fib": f, "blk": lax.rem(z + k, nz) * CORES + 1}
         pl.semaphore_signal(barrier, inc=1, device_id=device, device_id_type=MESH)
-    for device in z_peers:
-        pl.semaphore_signal(barrier, inc=1, device_id=device, device_id_type=MESH)
-    pl.semaphore_wait(barrier, plane - 1 + nz - 1)
+    pair = {"fib": f, "blk": twin}
+
+    @pl.when(core == 0)
+    def _():
+        pl.semaphore_wait(barrier, plane - 1)
+        pl.semaphore_signal(plane_in, inc=1, device_id=pair, device_id_type=MESH)
+
+    @pl.when(core == 1)
+    def _():
+        pl.semaphore_wait(plane_in, 1)
 
     for u in range(4):
         owner = owner_of(u, shift, side)
@@ -177,6 +192,16 @@
     rbuf[t] = part[t]
     fhigh[3], flow[3] = halves(fbuf[1, 1])
     rest = pl.ds(0, plane - 1)
+
+    @pl.when(core == 1)
+    def _():
+        pl.semaphore_wait(barrier, CORES * (nz - 1))
+        pl.semaphore_signal(z_in, inc=1, device_id=pair, device_id_type=MESH)
+
+    @pl.when(core == 0)
+    def _():
+        pl.semaphore_wait(z_in, 1)
+
     pltpu.make_async_copy(rbuf.at[rest], rbuf.at[rest], r_recv).wait()
     tile = jnp.sum(rbuf[...], axis=0)
     zsrc[...] = tile
@@ -302,6 +327,7 @@
                 pltpu.VMEM((nf, 2, 2, share, width_y), f32),
                 pltpu.VMEM((nf, share, 128), f32),
                 dma, dma((5,)), dma, dma, dma, dma, dma, dma, dma, dma, dma, dma, dma, dma, dma, dma, dma,
+                pltpu.SemaphoreType.REGULAR, pltpu.SemaphoreType.REGULAR,
             ],
             compiler_params=pltpu.CompilerParams(collective_id=0, has_side_effects=True, vmem_limit_bytes=48 << 20),
             cost_estimate=pl.CostEstimate(flops=2_000_000_000, bytes_accessed=5_000_000, transcendentals=64),

time: 70.2 us -> 69.3 us (0.987)
  Pallas kernels: 69.3 us -> 68.5 us
    pallas_call x1, Pallas kernels: 69.3 us -> 68.5 us  [shards(): pl.pallas_call(functools.partial(kernel, nf, nz), out_shape=jax.ShapeDtyp...]
where the time goes in v4:
time: 69.3 us; the launch traced here: 69.2 us
  Pallas kernels  68.5 us (99%)
  local copies, waits for them, and re-layouts  0.71 us (1%)
    pallas_call x1, Pallas kernels, shards(): pl.pallas_call(functools.partial(kernel, nf, nz), out_shape=jax.ShapeDtyp...  68.5 us

profile of v4, /device:TPU:1, one launch (start us, length us, event | category | flops | bytes accessed | tf_op | source)
XLA Modules:
  0.0 69.2 jit_solution(159304808713420978)
XLA Ops:
  0.0 68.5 %hosvd_step.1 = f32[33,2,4,256]{3,2,1,0:T(4,128)S(1)} custom-call(f32[33,2,32,256]{3,2,1,0:T(8,128)} %field.1, f32[64,512]{1,0:T(8,128)} %bitcast.1), custom_call_target="tpu_custom_call" | custom-call | flops 2000000000 | bytes 5000000 | tf_op jit(solution)/shard_map/hosvd_step/pallas_call | solution.py:307
  68.5 0.7 %copy.4 = f32[33,2,4,256]{3,2,1,0:T(4,128)} copy(f32[33,2,4,256]{3,2,1,0:T(4,128)S(1)} %hosvd_step.1) | data formatting | bytes 540672

commit v5 on v4

--- a/solution.py
+++ b/solution.py
@@ -10,6 +10,7 @@
 MESH = pl.DeviceIdType.MESH
 HIGHEST = lax.Precision.HIGHEST
 CORES = 2
+NN = (((1,), (0,)), ((), ()))
 NT = (((1,), (1,)), ((), ()))
 
 
@@ -63,7 +64,14 @@
     return high, (value - high.astype(jnp.float32)).astype(jnp.bfloat16)
 
 
-def kernel(nf, nz, field, start_hbm, out, start_t, fbuf, lbuf, fhigh, flow, lhigh, llow, part, extra, rbuf, zsrc, zbuf,
+def thirds(value):
+    high, rest = value.astype(jnp.bfloat16), value
+    rest = rest - high.astype(jnp.float32)
+    middle = rest.astype(jnp.bfloat16)
+    return high, middle, (rest - middle.astype(jnp.float32)).astype(jnp.bfloat16)
+
+
+def kernel(nf, nz, field, start_hbm, out, start_t, fbuf, lbuf, fparts, lparts, cbuf, part, extra, rbuf, zsrc, zbuf,
            gsrc, gbuf, osrc, lsrc, a_send, a_recv, own_sem, start_sem, l_send, l_recv, own_last, r_send, r_recv, z_send,
            z_recv, g_send, g_recv, o_send, o_recv, p_send, p_recv, plane_in, z_in):
     side = {16: 4, 4: 2}[nf]
@@ -160,7 +168,19 @@
         projected = jnp.dot(start_t[...], fibres, precision=HIGHEST, preferred_element_type=jnp.float32)
         return lax.dot_general(projected, fibres, NT, precision=HIGHEST, preferred_element_type=jnp.float32)
 
+    def times_halves(left, high, low, dims):
+        left_high, left_low = halves(left)
+        both = lax.dot_general(jnp.concatenate([left_high, left_low], axis=0), high, dims,
+                               preferred_element_type=jnp.float32)
+        return both[:rank] + both[rank:] + lax.dot_general(left_high, low, dims, preferred_element_type=jnp.float32)
+
+    def gram_term_halves(fibres):
+        high, low = halves(fibres)
+        projected = times_halves(start_t[...], high, low, NN)
+        return times_halves(projected, high, low, NT)
+
     extra[...] = jnp.zeros_like(extra)
+    lparts[...] = jnp.zeros_like(lparts)
     own.wait()
     start_copy.wait()
     chunks = [(0, 0, 0, 256), (0, 1, 0, 256), (1, 0, 0, 256), (1, 1, 0, 128), (1, 1, 128, 128)]
@@ -168,9 +188,12 @@
     for q, (s, zz, first, width) in enumerate(chunks):
         whole = fbuf.at[s, zz, :, pl.ds(first, width)]
         pltpu.make_async_copy(whole.at[others, :], whole.at[others, :], a_recv.at[q]).wait()
-        raw_t = raw_t + gram_term(whole[...])
+        if q < 4:
+            raw_t = raw_t + gram_term(whole[...])
+        else:
+            raw_t = gram_term_halves(whole[...])
         if q < 3:
-            fhigh[q], flow[q] = halves(whole[...])
+            fparts[q, 0], fparts[q, 1], fparts[q, 2] = thirds(whole[...])
         if q == 1:
             @pl.when(is_owner)
             def _():
@@ -179,18 +202,17 @@
                 term = gram_term(lbuf[...])
                 for n, (i, j) in enumerate(tiles):
                     extra[n] = term[8 * i : 8 * i + 8, 128 * j : 128 * j + 128]
-                lhigh[...], llow[...] = halves(lbuf[...])
+                lparts[0], lparts[1], lparts[2] = thirds(lbuf[...])
         if q == 3:
             for n, (i, j) in enumerate(tiles):
                 part[n] = raw_t[8 * i : 8 * i + 8, 128 * j : 128 * j + 128] + extra[n]
-            raw_t = jnp.zeros((rank, full_x), jnp.float32)
     for n, (i, j) in enumerate(tiles):
         part[n] += raw_t[8 * i : 8 * i + 8, 128 * j : 128 * j + 128]
 
     for other, device in plane_peers:
         pltpu.make_async_remote_copy(part.at[other], rbuf.at[t], r_send, r_recv, device, MESH).start()
     rbuf[t] = part[t]
-    fhigh[3], flow[3] = halves(fbuf[1, 1])
+    fparts[3, 0], fparts[3, 1], fparts[3, 2] = thirds(fbuf[1, 1])
     rest = pl.ds(0, plane - 1)
 
     @pl.when(core == 1)
@@ -219,33 +241,38 @@
     total_t = jnp.concatenate(
         [jnp.concatenate([gbuf[i * tiles_x + j] for j in range(tiles_x)], axis=1) for i in range(rank // 8)], axis=0)
 
-    def pad(count):
-        return [jnp.zeros((count, full_x), jnp.float32)] if count else []
-
-    inner = lax.dot_general(total_t, jnp.concatenate([total_t] + pad(128 - rank), axis=0), NT, precision=HIGHEST,
+    share = rank // nf
+    high, middle, low = thirds(total_t)
+    stack = jnp.concatenate([high, middle, low], axis=0)
+
+    def products(parts):
+        first = jnp.dot(stack, parts[0], preferred_element_type=jnp.float32)
+        second = jnp.dot(stack[: 2 * rank], parts[1], preferred_element_type=jnp.float32)
+        third = jnp.dot(high, parts[2], preferred_element_type=jnp.float32)
+        return first[:rank] + (second[:rank] + first[rank : 2 * rank]) + (
+            third + second[rank:] + first[2 * rank :])
+
+    padding = jnp.zeros((128 - rank, full_x), jnp.float32)
+    inner = lax.dot_general(total_t, jnp.concatenate([total_t, padding], axis=0), NT, precision=HIGHEST,
                             preferred_element_type=jnp.float32)
+    for q in range(4):
+        cbuf[:, 256 * q : 256 * q + 256] = products(fparts[q])
+    cbuf[:, 1024:] = products(lparts[...])
     inverse = eliminate(inner, rank)
-    basis_t = jnp.dot(inverse, jnp.concatenate(pad(rank) + [total_t] + pad(128 - 2 * rank), axis=0), precision=HIGHEST,
-                      preferred_element_type=jnp.float32)
-    basis_high, basis_low = halves(basis_t)
-    basis_both = jnp.concatenate([basis_high, basis_low], axis=0)
-
-    share = rank // nf
-
-    def core_of(high, low):
-        both = jnp.dot(basis_both, high, preferred_element_type=jnp.float32)
-        return both[:rank] + both[rank:] + jnp.dot(basis_high, low, preferred_element_type=jnp.float32)
-
-    @pl.when(is_owner)
-    def _():
-        core_part = core_of(lhigh[...], llow[...])
-        for j in range(nf):
-            lsrc[j] = core_part[share * j : share * j + share, :]
+
+    def core_of(lanes, width):
+        pieces = [jnp.zeros((rank, width), jnp.float32), cbuf[:, lanes]]
+        if 128 - 2 * rank:
+            pieces.append(jnp.zeros((128 - 2 * rank, width), jnp.float32))
+        return jnp.dot(inverse, jnp.concatenate(pieces, axis=0), precision=HIGHEST, preferred_element_type=jnp.float32)
 
     for q in range(4):
-        core_part = core_of(fhigh[q], flow[q])
+        core_part = core_of(pl.ds(256 * q, 256), 256)
         for j in range(nf):
             osrc[j, q // 2, q % 2] = core_part[share * j : share * j + share, :]
+    core_part = core_of(pl.ds(1024, 128), 128)
+    for j in range(nf):
+        lsrc[j] = core_part[share * j : share * j + share, :]
     target = out.at[pl.ds(2 * f, 2)]
     last_lanes = pl.ds(pl.multiple_of(lax.rem(row_unit, 2) * 128, 128), 128)
     last_target = out.at[last, lax.div(row_unit, 2), :, last_lanes]
@@ -313,10 +340,9 @@
                 pltpu.VMEM((rank, full_x), f32),
                 pltpu.VMEM((2, 2, full_x, width_y), f32),
                 pltpu.VMEM((full_x, 128), f32),
-                pltpu.VMEM((4, full_x, width_y), bf16),
-                pltpu.VMEM((4, full_x, width_y), bf16),
-                pltpu.VMEM((full_x, 128), bf16),
-                pltpu.VMEM((full_x, 128), bf16),
+                pltpu.VMEM((4, 3, full_x, width_y), bf16),
+                pltpu.VMEM((3, full_x, 128), bf16),
+                pltpu.VMEM((rank, 4 * width_y + 128), f32),
                 pltpu.VMEM((tiles, 8, 128), f32),
                 pltpu.VMEM((tiles, 8, 128), f32),
                 pltpu.VMEM((tiles, 8, 128), f32),

time: 69.3 us -> 68.5 us (0.988)
  Pallas kernels: 68.5 us -> 67.6 us
    pallas_call x1, Pallas kernels: 68.5 us -> 67.6 us  [shards(): pl.pallas_call(functools.partial(kernel, nf, nz), out_shape=jax.ShapeDtyp...]
where the time goes in v5:
time: 68.5 us; the launch traced here: 68.4 us
  Pallas kernels  67.6 us (99%)
  local copies, waits for them, and re-layouts  0.71 us (1%)
    pallas_call x1, Pallas kernels, shards(): pl.pallas_call(functools.partial(kernel, nf, nz), out_shape=jax.ShapeDtyp...  67.6 us

profile of v5, /device:TPU:1, one launch (start us, length us, event | category | flops | bytes accessed | tf_op | source)
XLA Modules:
  0.0 68.4 jit_solution(4962709384624400083)
XLA Ops:
  0.0 67.6 %hosvd_step.1 = f32[33,2,4,256]{3,2,1,0:T(4,128)S(1)} custom-call(f32[33,2,32,256]{3,2,1,0:T(8,128)} %field.1, f32[64,512]{1,0:T(8,128)} %bitcast.1), custom_call_target="tpu_custom_call" | custom-call | flops 2000000000 | bytes 5000000 | tf_op jit(solution)/shard_map/hosvd_step/pallas_call | solution.py:334
  67.7 0.7 %copy.4 = f32[33,2,4,256]{3,2,1,0:T(4,128)} copy(f32[33,2,4,256]{3,2,1,0:T(4,128)S(1)} %hosvd_step.1) | data formatting | bytes 540672

commit v6 on v5

--- a/solution.py
+++ b/solution.py
@@ -71,7 +71,7 @@
     return high, middle, (rest - middle.astype(jnp.float32)).astype(jnp.bfloat16)
 
 
-def kernel(nf, nz, field, start_hbm, out, start_t, fbuf, lbuf, fparts, lparts, cbuf, part, extra, rbuf, zsrc, zbuf,
+def kernel(nf, nz, field, start_hbm, out, start_t, fbuf, lbuf, fparts, lparts, cparts, part, extra, rbuf, zsrc, zbuf,
            gsrc, gbuf, osrc, lsrc, a_send, a_recv, own_sem, start_sem, l_send, l_recv, own_last, r_send, r_recv, z_send,
            z_recv, g_send, g_recv, o_send, o_recv, p_send, p_recv, plane_in, z_in):
     side = {16: 4, 4: 2}[nf]
@@ -90,11 +90,6 @@
     mine = pl.ds(pl.multiple_of(f * width_x, width_x), width_x)
     others = pl.ds(0, (nf - 1) * width_x)
 
-    own = pltpu.make_async_copy(field.at[pl.ds(2 * f, 2)], fbuf.at[:, :, mine, :], own_sem)
-    own.start()
-    start_copy = pltpu.make_async_copy(start_hbm, start_t, start_sem)
-    start_copy.start()
-
     steps = [(dy, dx) for dy in range(side) for dx in range(side)]
     steps.sort(key=lambda s: -ring_distance(s[0], side) - ring_distance(s[1], side))
     row_at = [lax.rem(row + d, side) * side for d in range(side)]
@@ -123,6 +118,11 @@
         pl.semaphore_signal(barrier, inc=1, device_id=device, device_id_type=MESH)
     pair = {"fib": f, "blk": twin}
 
+    own = pltpu.make_async_copy(field.at[pl.ds(2 * f, 2)], fbuf.at[:, :, mine, :], own_sem)
+    own.start()
+    start_copy = pltpu.make_async_copy(start_hbm, start_t, start_sem)
+    start_copy.start()
+
     @pl.when(core == 0)
     def _():
         pl.semaphore_wait(barrier, plane - 1)
@@ -131,18 +131,6 @@
     @pl.when(core == 1)
     def _():
         pl.semaphore_wait(plane_in, 1)
-
-    for u in range(4):
-        owner = owner_of(u, shift, side)
-        source = field.at[last, u // 2, :, pl.ds((u % 2) * 128, 128)]
-
-        @pl.when(owner != f)
-        def _():
-            pltpu.make_async_remote_copy(source, lbuf.at[mine, :], l_send, l_recv, {"fib": owner, "blk": b}, MESH).start()
-
-        @pl.when(owner == f)
-        def _():
-            pltpu.make_async_copy(source, lbuf.at[mine, :], own_last).start()
 
     def send_pair(q, _):
         s, zz = lax.div(q, 2), lax.rem(q, 2)
@@ -152,7 +140,20 @@
             ).start()
         return 0
 
-    lax.fori_loop(0, 3, send_pair, 0)
+    send_pair(0, 0)
+    for u in range(4):
+        owner = owner_of(u, shift, side)
+        source = field.at[last, u // 2, :, pl.ds((u % 2) * 128, 128)]
+
+        @pl.when(owner != f)
+        def _():
+            pltpu.make_async_remote_copy(source, lbuf.at[mine, :], l_send, l_recv, {"fib": owner, "blk": b}, MESH).start()
+
+        @pl.when(owner == f)
+        def _():
+            pltpu.make_async_copy(source, lbuf.at[mine, :], own_last).start()
+
+    lax.fori_loop(1, 3, send_pair, 0)
     for h in range(2):
         lanes = pl.ds(128 * h, 128)
         for peer in fib_peers:
@@ -181,6 +182,7 @@
 
     extra[...] = jnp.zeros_like(extra)
     lparts[...] = jnp.zeros_like(lparts)
+    cparts[...] = jnp.zeros_like(cparts)
     own.wait()
     start_copy.wait()
     chunks = [(0, 0, 0, 256), (0, 1, 0, 256), (1, 0, 0, 256), (1, 1, 0, 128), (1, 1, 128, 128)]
@@ -245,32 +247,30 @@
     high, middle, low = thirds(total_t)
     stack = jnp.concatenate([high, middle, low], axis=0)
 
-    def products(parts):
-        first = jnp.dot(stack, parts[0], preferred_element_type=jnp.float32)
-        second = jnp.dot(stack[: 2 * rank], parts[1], preferred_element_type=jnp.float32)
-        third = jnp.dot(high, parts[2], preferred_element_type=jnp.float32)
+    def products(parts, dims=NN, stack=stack):
+        first = lax.dot_general(stack, parts[0], dims, preferred_element_type=jnp.float32)
+        second = lax.dot_general(stack[: 2 * rank], parts[1], dims, preferred_element_type=jnp.float32)
+        third = lax.dot_general(stack[:rank], parts[2], dims, preferred_element_type=jnp.float32)
         return first[:rank] + (second[:rank] + first[rank : 2 * rank]) + (
             third + second[rank:] + first[2 * rank :])
 
     padding = jnp.zeros((128 - rank, full_x), jnp.float32)
-    inner = lax.dot_general(total_t, jnp.concatenate([total_t, padding], axis=0), NT, precision=HIGHEST,
-                            preferred_element_type=jnp.float32)
+    zeros_right = padding.astype(jnp.bfloat16)
+    wide = [jnp.concatenate([value, zeros_right], axis=0) for value in (high, middle, low)]
+    inner = products(wide, NT)
     for q in range(4):
-        cbuf[:, 256 * q : 256 * q + 256] = products(fparts[q])
-    cbuf[:, 1024:] = products(lparts[...])
-    inverse = eliminate(inner, rank)
-
-    def core_of(lanes, width):
-        pieces = [jnp.zeros((rank, width), jnp.float32), cbuf[:, lanes]]
-        if 128 - 2 * rank:
-            pieces.append(jnp.zeros((128 - 2 * rank, width), jnp.float32))
-        return jnp.dot(inverse, jnp.concatenate(pieces, axis=0), precision=HIGHEST, preferred_element_type=jnp.float32)
+        cparts[:, rank : 2 * rank, 256 * q : 256 * q + 256] = jnp.stack(thirds(products(fparts[q])))
+    cparts[:, rank : 2 * rank, 1024:] = jnp.stack(thirds(products(lparts[...])))
+    inverse = jnp.concatenate(thirds(eliminate(inner, rank)), axis=0)
+
+    def core_of(lanes):
+        return products(cparts[:, :, lanes], NN, inverse)
 
     for q in range(4):
-        core_part = core_of(pl.ds(256 * q, 256), 256)
+        core_part = core_of(pl.ds(256 * q, 256))
         for j in range(nf):
             osrc[j, q // 2, q % 2] = core_part[share * j : share * j + share, :]
-    core_part = core_of(pl.ds(1024, 128), 128)
+    core_part = core_of(pl.ds(1024, 128))
     for j in range(nf):
         lsrc[j] = core_part[share * j : share * j + share, :]
     target = out.at[pl.ds(2 * f, 2)]
@@ -342,7 +342,7 @@
                 pltpu.VMEM((full_x, 128), f32),
                 pltpu.VMEM((4, 3, full_x, width_y), bf16),
                 pltpu.VMEM((3, full_x, 128), bf16),
-                pltpu.VMEM((rank, 4 * width_y + 128), f32),
+                pltpu.VMEM((3, 128, 4 * width_y + 128), bf16),
                 pltpu.VMEM((tiles, 8, 128), f32),
                 pltpu.VMEM((tiles, 8, 128), f32),
                 pltpu.VMEM((tiles, 8, 128), f32),

time: 68.5 us -> 68.2 us (level)
  no operation moved by 1% of the time
where the time goes in v6:
time: 68.2 us; the launch traced here: 68.1 us
  Pallas kernels  67.3 us (99%)
  local copies, waits for them, and re-layouts  0.71 us (1%)
    pallas_call x1, Pallas kernels, shards(): pl.pallas_call(functools.partial(kernel, nf, nz), out_shape=jax.ShapeDtyp...  67.3 us

profile of v6, /device:TPU:1, one launch (start us, length us, event | category | flops | bytes accessed | tf_op | source)
XLA Modules:
  0.0 68.1 jit_solution(6427267125060438513)
XLA Ops:
  0.0 67.3 %hosvd_step.1 = f32[33,2,4,256]{3,2,1,0:T(4,128)S(1)} custom-call(f32[33,2,32,256]{3,2,1,0:T(8,128)} %field.1, f32[64,512]{1,0:T(8,128)} %bitcast.1), custom_call_target="tpu_custom_call" | custom-call | flops 2000000000 | bytes 5000000 | tf_op jit(solution)/shard_map/hosvd_step/pallas_call | solution.py:334
  67.3 0.7 %copy.4 = f32[33,2,4,256]{3,2,1,0:T(4,128)} copy(f32[33,2,4,256]{3,2,1,0:T(4,128)S(1)} %hosvd_step.1) | data formatting | bytes 540672

commit v7 on v6

--- a/solution.py
+++ b/solution.py
@@ -276,13 +276,20 @@
     target = out.at[pl.ds(2 * f, 2)]
     last_lanes = pl.ds(pl.multiple_of(lax.rem(row_unit, 2) * 128, 128), 128)
     last_target = out.at[last, lax.div(row_unit, 2), :, last_lanes]
-    for peer in fib_peers:
-        device = {"fib": peer, "blk": b}
-        pltpu.make_async_remote_copy(osrc.at[peer], target, o_send, o_recv, device, MESH).start()
-
-        @pl.when(is_owner)
-        def _():
-            pltpu.make_async_remote_copy(lsrc.at[peer], last_target, p_send, p_recv, device, MESH).start()
+    def send_core(with_last):
+        for peer in fib_peers:
+            device = {"fib": peer, "blk": b}
+            pltpu.make_async_remote_copy(osrc.at[peer], target, o_send, o_recv, device, MESH).start()
+            if with_last:
+                pltpu.make_async_remote_copy(lsrc.at[peer], last_target, p_send, p_recv, device, MESH).start()
+
+    @pl.when(is_owner)
+    def _():
+        send_core(True)
+
+    @pl.when(jnp.logical_not(is_owner))
+    def _():
+        send_core(False)
 
     own_core = pltpu.make_async_copy(osrc.at[f], target, own_sem)
     own_core.start()

time: 68.2 us -> 68.2 us (level)
  no operation moved by 1% of the time
where the time goes in v7:
time: 68.2 us; the launch traced here: 68.1 us
  Pallas kernels  67.3 us (99%)
  local copies, waits for them, and re-layouts  0.71 us (1%)
    pallas_call x1, Pallas kernels, shards(): pl.pallas_call(functools.partial(kernel, nf, nz), out_shape=jax.ShapeDtyp...  67.3 us

profile of v7, /device:TPU:1, one launch (start us, length us, event | category | flops | bytes accessed | tf_op | source)
XLA Modules:
  0.0 68.1 jit_solution(4098223263375638639)
XLA Ops:
  0.0 67.3 %hosvd_step.1 = f32[33,2,4,256]{3,2,1,0:T(4,128)S(1)} custom-call(f32[33,2,32,256]{3,2,1,0:T(8,128)} %field.1, f32[64,512]{1,0:T(8,128)} %bitcast.1), custom_call_target="tpu_custom_call" | custom-call | flops 2000000000 | bytes 5000000 | tf_op jit(solution)/shard_map/hosvd_step/pallas_call | solution.py:341
  67.3 0.7 %copy.4 = f32[33,2,4,256]{3,2,1,0:T(4,128)} copy(f32[33,2,4,256]{3,2,1,0:T(4,128)S(1)} %hosvd_step.1) | data formatting | bytes 540672
